TPU v7x, 256 devices: a whole 4x4x8 slice. The times are simulated.
256 devices in a mesh: dp: 64 (over x, z, y_lo), mp: 4 (over y_hi, core).
Axes of the slice: x: 4, y: 4 (y_hi: 2, y_lo: 2; y = y_hi * 2 + y_lo), z: 8, core: 2. Of those that a mesh axis runs over, the one named last changes fastest.
Arguments:
- gate_pre: bfloat16 [16384, 12288], P('dp', 'mp'), may hold values from -6 to 6
- up_pre: bfloat16 [16384, 12288], P('dp', 'mp'), may hold values from -16 to 16
- out_grad: bfloat16 [16384, 3072], P('dp', 'mp'), may hold values from -0.046875 to 0.046875
Outputs:
- weight_grad: bfloat16 [12288, 3072], P(('mp', 'dp'))
All inputs are finite; a program needn't handle non-finite values.
Results may differ from a plain program's by a relative error of at most 0.0049.
Values may be sent and summed in bfloat16 or wider, within the bound.
A program may use at most 128 MiB of HBM per device.

v0:
```python
import jax
import jax.numpy as jnp
from jax import lax
from jax.sharding import PartitionSpec as P


def per_device(gate_pre, up_pre, out_grad):
    hidden = (jax.nn.silu(gate_pre.astype(jnp.float32)) * up_pre.astype(jnp.float32)).astype(
        jnp.bfloat16
    )
    full_grad = lax.all_gather(out_grad, "mp", axis=1, tiled=True)
    contract = (((0,), (0,)), ((), ()))
    products = lax.dot_general(hidden, full_grad, contract, preferred_element_type=jnp.float32)
    summed = lax.psum_scatter(products, "dp", scatter_dimension=0, tiled=True)
    return summed.astype(jnp.bfloat16)


def solution(mesh):
    in_specs = (P("dp", "mp"), P("dp", "mp"), P("dp", "mp"))
    out_specs = P(("mp", "dp"), None)
    return jax.shard_map(
        per_device, mesh=mesh, in_specs=in_specs, out_specs=out_specs, check_vma=False
    )
```

profile of v0, /device:TPU:8, one launch (start us, length us, event | category | flops | bytes accessed | tf_op | source)
XLA Modules:
  0.0 872.7 jit_solution(5259307954306815577)
XLA Ops:
  6.5 0.0 all-gather.2.cloned.1.call-start
  6.5 0.7 all-gather.2.cloned.1.call-update
  7.3 0.0 reduce-scatter.2.cloned.1.call-start
  7.3 30.1 %all-gather.2.cloned.1.call-done = bf16[256,3072]{1,0:T(8,128)(2,1)} async-done(((bf16[256,768]{1,0:T(8,128)(2,1)}), bf16[256,3072]{1,0:T(8,128)(2,1)}) %all-gather.2.cloned.1.call-update) | async-done | bytes 1572880 | tf_op jit(solution)/shard_map/all_gather | solution.py:11
  37.4 16.8 %fusion.5 = f32[3072,3072]{1,0:T(8,128)} fusion(bf16[256,3072]{1,0:T(8,128)(2,1)} %all-gather.2.cloned.1.call-done, bf16[256,3072]{1,0:T(8,128)(2,1)} %param.4, bf16[256,3072]{1,0:T(8,128)(2,1)} %param.3), kind=kOutput, calls=%fused_computation.7 | convolution fusion | flops 4838129664 | bytes 42467328 | tf_op jit(solution)/shard_map/dot_general | solution.py:13
  54.2 0.0 reduce-scatter.2.cloned.1.call-update
  54.2 809.8 %reduce-scatter.2.cloned.1.call-done = f32[48,3072]{1,0:T(8,128)} async-done(((f32[3072,3072]{1,0:T(8,128)}), f32[48,3072]{1,0:T(8,128)}) %reduce-scatter.2.cloned.1.call-update) | async-done | bytes 589840 | tf_op jit(solution)/shard_map/reduce_scatter | solution.py:14
  864.1 1.8 convert_element_type.15
Async XLA Ops:
  6.5 30.9 %all-gather.2.cloned.1.call-start = ((), (), s32[]{:S(2)}) async-start(), calls=%async_computation.1 | async-start | bytes 1966080 | tf_op jit(solution)/shard_map/all_gather | solution.py:11
  7.3 856.8 %reduce-scatter.2.cloned.1.call-start = ((), (), s32[]{:S(2)}) async-start(), calls=%async_computation.2 | async-start | bytes 38338560 | tf_op jit(solution)/shard_map/reduce_scatter | solution.py:14
Sparse Core Ops, SparseCore 0:
  9.1 28.2 all-gather.1
  54.4 809.6 reduce-scatter.1
where the time goes:
time: 876 us; the launch traced here: 873 us
  waiting for transfers between devices  841 us (96%)
  matrix products  16.8 us (2%)
  between operations  13.4 us (2%)
    reduce_scatter x1, waiting for transfers between devices, per_device(): summed = lax.psum_scatter(products, 'dp', scatter_dimension=0, tiled=True)  810 us
    all_gather x1, waiting for transfers between devices, per_device(): full_grad = lax.all_gather(out_grad, 'mp', axis=1, tiled=True)  30.1 us
  transfers between devices with their start and end apart: 2, of which 2 were waited for; matrix products, arithmetic and copies ran while one was open for 0% of the time, Pallas kernels for 0%

commit v1 on v0

v1 whole, which is shorter than its diff:
```python
import functools

import jax
import jax.numpy as jnp
from jax import lax
from jax.experimental import pallas as pl
from jax.experimental.pallas import tpu as pltpu
from jax.sharding import PartitionSpec as P

MESH = pl.DeviceIdType.MESH
NX = 4
NZ = 8
OWN, LEFT, RIGHT, OPP = range(4)


def kernel(
    dims,
    gate_hbm,
    up_hbm,
    og_hbm,
    out_ref,
    gate,
    up,
    ht,
    hbuf,
    hrel,
    gbuf,
    zs,
    zr,
    fin,
    ys,
    yr,
    loc_sem,
    og_sem,
    gs_sem,
    gr_sem,
    gp_sem,
    cs_sem,
    cr_sem,
    hs_sem,
    hr_sem,
    zs_sem,
    zr_sem,
    ys_sem,
    yr_sem,
):
    tb, rows, w, nu, nz = dims
    far = nz // 2
    half_t = tb // 2
    dp, mp = lax.axis_index("dp"), lax.axis_index("mp")
    y = lax.rem(dp, 2)
    z = lax.rem(dp // 2, nz)
    x = dp // (2 * nz)
    core = lax.rem(mp, 2)
    half = mp // 2

    def at(xx, zz):
        return ((lax.rem(xx, NX) * nz + lax.rem(zz, nz)) * 2 + y, mp)

    right, left = at(x + 1, z), at(x + NX - 1, z)
    zright, zleft = at(x, z + 1), at(x, z + nz - 1)
    ypeer = (dp + 1 - 2 * y, mp)
    partner = (dp, mp + 1 - 2 * core)
    cross = (dp, mp + 2 - 4 * half)
    peers = (right, left, zright, zleft, ypeer, partner, cross)

    def unit(t, u, who):
        return (t * nu + u) * 2 + who

    def rcopy(src, dst, ssem, rsem, to):
        return pltpu.make_async_remote_copy(
            src_ref=src, dst_ref=dst, send_sem=ssem, recv_sem=rsem, device_id=to, device_id_type=MESH
        )

    ncol = gate.shape[0]
    wide = gate.shape[2]
    gate_copies = [
        pltpu.make_async_copy(gate_hbm.at[:, pl.ds(i * wide, wide)], gate.at[i], loc_sem.at[0, i]) for i in range(ncol)
    ]
    up_copies = [
        pltpu.make_async_copy(up_hbm.at[:, pl.ds(i * wide, wide)], up.at[i], loc_sem.at[1, i]) for i in range(ncol)
    ]
    og_copies = [
        pltpu.make_async_copy(og_hbm.at[:, pl.ds(u * w, w)], gbuf.at[unit(0, u, 0), OWN], og_sem.at[u])
        for u in range(nu)
    ]
    for c in og_copies + gate_copies + up_copies:
        c.start()

    barrier = pltpu.get_barrier_semaphore()
    for peer in peers:
        pl.semaphore_signal(barrier, inc=1, device_id=peer, device_id_type=MESH)
    pl.semaphore_wait(barrier, len(peers))

    FIRST, LAST = pl.ds(0, half_t), pl.ds(half_t, half_t)

    def g_own(t, u, i):
        k = t * nu + u
        src = gbuf.at[unit(t, u, 0), OWN]
        if i == 0:
            return rcopy(src, gbuf.at[unit(t, u, 0), LEFT], gs_sem.at[0, k], gr_sem.at[0, k], right)
        if i == 1:
            return rcopy(src, gbuf.at[unit(t, u, 0), RIGHT], gs_sem.at[1, k], gr_sem.at[1, k], left)
        return rcopy(src, gbuf.at[unit(t, u, 1), OWN], gs_sem.at[2, k], gp_sem.at[0, k], partner)

    def g_relay(t, u, i):
        k = t * nu + u
        own = unit(t, u, 0)
        if i == 0:
            return rcopy(
                gbuf.at[own, LEFT, FIRST], gbuf.at[own, OPP, FIRST], gs_sem.at[3, k], gr_sem.at[2, k], right
            )
        return rcopy(gbuf.at[own, RIGHT, LAST], gbuf.at[own, OPP, LAST], gs_sem.at[4, k], gr_sem.at[3, k], left)

    def g_give(t, u, i):
        k = t * nu + u
        own, his = unit(t, u, 0), unit(t, u, 1)
        if i < 2:
            slot = (LEFT, RIGHT)[i]
            return rcopy(gbuf.at[own, slot], gbuf.at[his, slot], gs_sem.at[5 + i, k], gp_sem.at[1 + i, k], partner)
        part = (FIRST, LAST)[i - 2]
        return rcopy(
            gbuf.at[own, OPP, part], gbuf.at[his, OPP, part], gs_sem.at[5 + i, k], gp_sem.at[1 + i, k], partner
        )

    def g_cross(u):
        return rcopy(
            gbuf.at[unit(0, u, 0), OWN], gbuf.at[unit(1, u, 0), OWN], cs_sem.at[u], cr_sem.at[u], cross
        )

    def send_own(t):
        def body(u, _):
            if t == 1:
                g_cross(u).wait_recv()
            for i in range(3):
                g_own(t, u, i).start()
            return 0

        lax.fori_loop(0, nu, body, 0)

    def relay(t):
        def body(u, _):
            g_own(t, u, 0).wait_recv()
            g_relay(t, u, 0).start()
            g_give(t, u, 0).start()
            g_own(t, u, 1).wait_recv()
            g_relay(t, u, 1).start()
            g_give(t, u, 1).start()
            return 0

        lax.fori_loop(0, nu, body, 0)

    def give_opp(t):
        def body(u, _):
            for i in range(2):
                g_relay(t, u, i).wait_recv()
                g_give(t, u, 2 + i).start()
            return 0

        lax.fori_loop(0, nu, body, 0)

    def z_of(o):
        odd = lax.rem(o, 2)
        rel = odd * (far - (o + 1) // 2) + (1 - odd) * (far + o // 2)
        return lax.rem(z + rel, nz)

    xr, xl, xo = lax.rem(x + 1, NX), lax.rem(x + NX - 1, NX), lax.rem(x + 2, NX)

    def h_copy(o, i):
        zi = z_of(o)
        if i == 0:
            pair, to = (ht.at[xr, zi], hbuf.at[0, zi]), right
        elif i == 1:
            pair, to = (ht.at[xl, zi], hbuf.at[1, zi]), left
        elif i == 2:
            pair, to = (ht.at[xo, zi, 0], hrel.at[0, zi]), right
        elif i == 3:
            pair, to = (ht.at[xo, zi, 1], hrel.at[1, zi]), left
        elif i == 4:
            pair, to = (hrel.at[0, zi], hbuf.at[2, zi, 0]), right
        else:
            pair, to = (hrel.at[1, zi], hbuf.at[2, zi, 1]), left
        return rcopy(pair[0], pair[1], hs_sem.at[i, o], hr_sem.at[i, o], to)

    def h_send(lo, hi):
        def body(o, _):
            for i in range(4):
                h_copy(o, i).start()
            return 0

        lax.fori_loop(lo, hi, body, 0)

    def h_relay(lo, hi):
        def body(o, _):
            for i in range(2):
                h_copy(o, 2 + i).wait_recv()
                h_copy(o, 4 + i).start()
            return 0

        lax.fori_loop(lo, hi, body, 0)

    def h_wait(lo, hi):
        def body(o, _):
            for i in (0, 1, 4, 5):
                h_copy(o, i).wait_recv()
            return 0

        lax.fori_loop(lo, hi, body, 0)

    def z_copy(direction, d, n):
        to = (zright, zleft)[direction]
        if d == far:
            src, dst = zs.at[direction, d - 1, n, direction], zr.at[direction, d - 1, n, direction]
        else:
            src, dst = zs.at[direction, d - 1, n], zr.at[direction, d - 1, n]
        return rcopy(src, dst, zs_sem.at[direction, d - 1, n], zr_sem.at[direction, d - 1, n], to)

    def y_copy(n):
        return rcopy(ys.at[n], yr.at[n], ys_sem.at[n], yr_sem.at[n], ypeer)

    def lhs(slot, zi):
        block = ht[x, zi] if slot == OWN else hbuf[slot - 1, zi]
        return block.reshape(2 * rows, tb)

    def product(n, zis):
        total = None
        for slot in range(4):
            left_side = [lhs(slot, zi) for zi in zis]
            block = left_side[0] if len(zis) == 1 else jnp.concatenate(left_side, axis=0)
            term = jnp.dot(block, gbuf[n, slot], preferred_element_type=jnp.float32)
            total = term if total is None else total + term
        return total.reshape(len(zis), 2, rows, w)

    def step(n, d):
        if d == far:
            p = product(n, [lax.rem(z + far, nz)])
            for direction in range(2):
                zs[direction, d - 1, n, direction] = p[0, direction].astype(jnp.bfloat16)
                z_copy(direction, d, n).start()
        elif d > 0:
            p = product(n, [lax.rem(z + d, nz), lax.rem(z + nz - d, nz)])
            for direction in range(2):
                z_copy(direction, d + 1, n).wait_recv()
                if d + 1 == far:
                    zs[direction, d - 1, n, direction] = (
                        p[direction, direction] + zr[direction, d, n, direction].astype(jnp.float32)
                    ).astype(jnp.bfloat16)
                    zs[direction, d - 1, n, 1 - direction] = p[direction, 1 - direction].astype(jnp.bfloat16)
                else:
                    zs[direction, d - 1, n] = (p[direction] + zr[direction, d, n].astype(jnp.float32)).astype(
                        jnp.bfloat16
                    )
                z_copy(direction, d, n).start()
        else:
            p = product(n, [z])[0]
            for direction in range(2):
                z_copy(direction, 1, n).wait_recv()
                p = p + zr[direction, 0, n].astype(jnp.float32)
            fin[n] = p
            ys[n] = fin[n, 1 - y].astype(jnp.bfloat16)
            y_copy(n).start()

    def phase(t, d):
        def body(u, _):
            step(unit(t, u, 0), d)
            if d == far:
                g_own(t, u, 2).wait_recv()
                for i in range(4):
                    g_give(t, u, i).wait_recv()
            step(unit(t, u, 1), d)
            return 0

        lax.fori_loop(0, nu, body, 0)

    def finish(t):
        def body(u, _):
            for who in range(2):
                n = unit(t, u, who)
                y_copy(n).wait_recv()
                q = (
                    (half + t - 2 * half * t) * 2 + (core + who - 2 * core * who)
                )
                column = pl.multiple_of((q * nu + u) * w, w)
                out_ref[:, pl.ds(column, w)] = (fin[n, y] + yr[n].astype(jnp.float32)).astype(jnp.bfloat16)
            return 0

        lax.fori_loop(0, nu, body, 0)

    for c in og_copies:
        c.wait()
    send_own(0)

    def cross_body(u, _):
        g_cross(u).start()
        return 0

    lax.fori_loop(0, nu, cross_body, 0)

    def silu_body(i, _):
        pltpu.make_async_copy(gate_hbm.at[:, pl.ds(pl.multiple_of(i * wide, 128), wide)], gate.at[i], loc_sem.at[0, i]).wait()
        pltpu.make_async_copy(up_hbm.at[:, pl.ds(pl.multiple_of(i * wide, 128), wide)], up.at[i], loc_sem.at[1, i]).wait()
        g = gate[i].astype(jnp.float32)
        h = (g / (1.0 + jnp.exp(-g)) * up[i].astype(jnp.float32)).astype(jnp.bfloat16)
        ht[i // (nz * 2 * rows // wide), pl.ds(lax.rem(i, nz * 2 * rows // wide) * (wide // (2 * rows)), wide // (2 * rows))] = (
            h.T.reshape(wide // (2 * rows), 2, rows, tb)
        )
        return 0

    lax.fori_loop(0, ncol, silu_body, 0)

    h_send(0, 3)
    relay(0)
    h_relay(0, 3)
    h_send(3, nz)
    give_opp(0)
    h_wait(0, 1)
    phase(0, far)
    h_wait(1, 3)
    phase(0, far - 1)
    h_relay(3, 5)
    for d in range(far - 2, 0, -1):
        o = 2 * (far - d) - 1
        h_wait(o, o + 2)
        phase(0, d)
        if d == 2:
            h_relay(5, nz)
            send_own(1)
    relay(1)
    h_wait(nz - 1, nz)
    phase(0, 0)
    give_opp(1)
    for d in range(far, -1, -1):
        phase(1, d)
        if d == far:
            finish(0)
    finish(1)

    def drain_g(u, _):
        for t in range(2):
            for i in range(3):
                g_own(t, u, i).wait_send()
            for i in range(2):
                g_relay(t, u, i).wait_send()
            for i in range(4):
                g_give(t, u, i).wait_send()
        g_cross(u).wait_send()
        return 0

    lax.fori_loop(0, nu, drain_g, 0)

    def drain_h(o, _):
        for i in range(6):
            h_copy(o, i).wait_send()
        return 0

    lax.fori_loop(0, nz, drain_h, 0)

    def drain_z(n, _):
        for d in range(1, far + 1):
            for direction in range(2):
                z_copy(direction, d, n).wait_send()
        y_copy(n).wait_send()
        return 0

    lax.fori_loop(0, 4 * nu, drain_z, 0)


def run(gate_pre, up_pre, out_grad, w=256, nz=NZ, interpret=False):
    tb, hidden = gate_pre.shape
    rows = hidden // (NX * nz * 2)
    nu = out_grad.shape[1] // w
    features = 4 * out_grad.shape[1]
    far = nz // 2
    bf16 = jnp.bfloat16
    wide = 2 * rows * nz // 2
    ncol = hidden // wide
    n = 4 * nu
    dma = pltpu.SemaphoreType.DMA
    return pl.pallas_call(
        functools.partial(kernel, (tb, rows, w, nu, nz)),
        out_shape=jax.ShapeDtypeStruct((rows, features), bf16),
        in_specs=[pl.BlockSpec(memory_space=pl.ANY)] * 3,
        out_specs=pl.BlockSpec(memory_space=pltpu.VMEM),
        scratch_shapes=[
            pltpu.VMEM((ncol, tb, wide), bf16),
            pltpu.VMEM((ncol, tb, wide), bf16),
            pltpu.VMEM((NX, nz, 2, rows, tb), bf16),
            pltpu.VMEM((3, nz, 2, rows, tb), bf16),
            pltpu.VMEM((2, nz, rows, tb), bf16),
            pltpu.VMEM((n, 4, tb, w), bf16),
            pltpu.VMEM((2, far, n, 2, rows, w), bf16),
            pltpu.VMEM((2, far, n, 2, rows, w), bf16),
            pltpu.VMEM((n, 2, rows, w), jnp.float32),
            pltpu.VMEM((n, rows, w), bf16),
            pltpu.VMEM((n, rows, w), bf16),
            dma((2, ncol)),
            dma((nu,)),
            dma((9, 2 * nu)),
            dma((4, 2 * nu)),
            dma((5, 2 * nu)),
            dma((nu,)),
            dma((nu,)),
            dma((6, nz)),
            dma((6, nz)),
            dma((2, far, n)),
            dma((2, far, n)),
            dma((n,)),
            dma((n,)),
        ],
        compiler_params=pltpu.CompilerParams(
            collective_id=0, has_side_effects=True, vmem_limit_bytes=60 * 1024 * 1024
        ),
        interpret=interpret,
    )(gate_pre, up_pre, out_grad)


def solution(mesh):
    return jax.shard_map(
        run,
        mesh=mesh,
        in_specs=(P("dp", "mp"), P("dp", "mp"), P("dp", "mp")),
        out_specs=P(("mp", "dp"), None),
        check_vma=False,
    )
```

time: 876 us -> 90.8 us (0.10)
  waiting for transfers between devices: 841 us -> 0 us
  Pallas kernels: 0 us -> 89 us
  matrix products: 16.8 us -> 0 us
  between operations: 13.4 us -> 0.01 us
    reduce_scatter x1 -> x0, waiting for transfers between devices: 810 us -> none  [per_device(): summed = lax.psum_scatter(products, 'dp', scatter_dimension=0, tiled=True)]
    pallas_call x0 -> x1, Pallas kernels: none -> 89 us  [run(): pl.pallas_call(functools.partial(kernel, (tb, rows, w, nu, nz)), out_shap...]
    all_gather x1 -> x0, waiting for transfers between devices: 30.1 us -> none  [per_device(): full_grad = lax.all_gather(out_grad, 'mp', axis=1, tiled=True)]
    dot_general x1 -> x0, matrix products: 16.8 us -> none  [per_device(): lax.dot_general(hidden, full_grad, contract, preferred_element_type=jnp.f...]
  transfers between devices with their start and end apart: 2 -> 0, of which waited for: 2 -> 0; matrix products, arithmetic and copies ran while one was open for 0% -> 0% of each run, Pallas kernels for 0% -> 0%
where the time goes in v1:
time: 90.8 us; the launch traced here: 90.7 us
  Pallas kernels  89 us (98%)
  local copies, waits for them, and re-layouts  1.69 us (2%)
    pallas_call x1, Pallas kernels, run(): pl.pallas_call(functools.partial(kernel, (tb, rows, w, nu, nz)), out_shap...  89 us

profile of v1, /device:TPU:8, one launch (start us, length us, event | category | flops | bytes accessed | tf_op | source)
XLA Modules:
  0.0 90.7 jit_solution(12699809551387660279)
XLA Ops:
  0.0 89.0 %shard_map.37 = bf16[48,3072]{1,0:T(8,128)(2,1)} custom-call(bf16[256,3072]{1,0:T(8,128)(2,1)} %gate_hbm.1, bf16[256,3072]{1,0:T(8,128)(2,1)} %up_hbm.1, bf16[256,768]{1,0:T(8,128)(2,1)} %og_hbm.1), custom_call_target="tpu_custom_call" | custom-call | tf_op jit(solution)/shard_map/pallas_call | solution.py:379
  89.0 1.7 %copy.5 = bf16[48,3072]{1,0:T(8,128)(2,1)} copy(bf16[48,3072]{1,0:T(8,128)(2,1)} %shard_map.37) | data formatting | bytes 589824

commit v2 on v1

--- a/solution.py
+++ b/solution.py
@@ -11,6 +11,8 @@
 NX = 4
 NZ = 8
 OWN, LEFT, RIGHT, OPP = range(4)
+Y_FIRST = ((1, 0), (1, 1))
+ACROSS = (1, 2)
 
 
 def kernel(
@@ -43,6 +45,12 @@
     zr_sem,
     ys_sem,
     yr_sem,
+    yps,
+    ypr,
+    yps_sem,
+    ypr_sem,
+    cxs_sem,
+    cxr_sem,
 ):
     tb, rows, w, nu, nz = dims
     far = nz // 2
@@ -128,36 +136,45 @@
             gbuf.at[unit(0, u, 0), OWN], gbuf.at[unit(1, u, 0), OWN], cs_sem.at[u], cr_sem.at[u], cross
         )
 
-    def send_own(t):
-        def body(u, _):
-            if t == 1:
-                g_cross(u).wait_recv()
-            for i in range(3):
-                g_own(t, u, i).start()
-            return 0
-
-        lax.fori_loop(0, nu, body, 0)
-
-    def relay(t):
-        def body(u, _):
-            g_own(t, u, 0).wait_recv()
-            g_relay(t, u, 0).start()
-            g_give(t, u, 0).start()
-            g_own(t, u, 1).wait_recv()
-            g_relay(t, u, 1).start()
-            g_give(t, u, 1).start()
-            return 0
-
-        lax.fori_loop(0, nu, body, 0)
-
-    def give_opp(t):
-        def body(u, _):
-            for i in range(2):
+    def g_across(u, i):
+        here, there = unit(0, u, 0), unit(1, u, 0)
+        if i < 2:
+            slot = (LEFT, RIGHT)[i]
+            src, dst = gbuf.at[here, slot], gbuf.at[there, slot]
+        else:
+            part = (FIRST, LAST)[i - 2]
+            src, dst = gbuf.at[here, OPP, part], gbuf.at[there, OPP, part]
+        return rcopy(src, dst, cxs_sem.at[i, u], cxr_sem.at[i, u], cross)
+
+    def across(t, u):
+        return t == 1 and u in ACROSS
+
+    def send_own(t, u):
+        if t == 1:
+            g_cross(u).wait_recv()
+        for i in (2,) if across(t, u) else (0, 1, 2):
+            g_own(t, u, i).start()
+
+    def relay(t, u):
+        for i in range(2):
+            if across(t, u):
+                g_across(u, i).wait_recv()
+            else:
+                g_own(t, u, i).wait_recv()
+                g_relay(t, u, i).start()
+            g_give(t, u, i).start()
+            if across(1 - t, u):
+                g_across(u, i).start()
+
+    def give_opp(t, u):
+        for i in range(2):
+            if across(t, u):
+                g_across(u, 2 + i).wait_recv()
+            else:
                 g_relay(t, u, i).wait_recv()
-                g_give(t, u, 2 + i).start()
-            return 0
-
-        lax.fori_loop(0, nu, body, 0)
+            g_give(t, u, 2 + i).start()
+            if across(1 - t, u):
+                g_across(u, 2 + i).start()
 
     def z_of(o):
         odd = lax.rem(o, 2)
@@ -182,9 +199,9 @@
             pair, to = (hrel.at[1, zi], hbuf.at[2, zi, 1]), left
         return rcopy(pair[0], pair[1], hs_sem.at[i, o], hr_sem.at[i, o], to)
 
-    def h_send(lo, hi):
+    def h_send(lo, hi, kinds):
         def body(o, _):
-            for i in range(4):
+            for i in kinds:
                 h_copy(o, i).start()
             return 0
 
@@ -218,18 +235,72 @@
     def y_copy(n):
         return rcopy(ys.at[n], yr.at[n], ys_sem.at[n], yr_sem.at[n], ypeer)
 
-    def lhs(slot, zi):
-        block = ht[x, zi] if slot == OWN else hbuf[slot - 1, zi]
-        return block.reshape(2 * rows, tb)
-
-    def product(n, zis):
+    def lhs(slot, zi, yi):
+        at_z = ht.at[x, zi] if slot == OWN else hbuf.at[slot - 1, zi]
+        return at_z[...].reshape(2 * rows, tb) if yi is None else at_z[yi]
+
+    def product(n, zis, yi=None):
         total = None
         for slot in range(4):
-            left_side = [lhs(slot, zi) for zi in zis]
+            left_side = [lhs(slot, zi, yi) for zi in zis]
             block = left_side[0] if len(zis) == 1 else jnp.concatenate(left_side, axis=0)
             term = jnp.dot(block, gbuf[n, slot], preferred_element_type=jnp.float32)
             total = term if total is None else total + term
-        return total.reshape(len(zis), 2, rows, w)
+        if yi is None:
+            return total.reshape(len(zis), 2, rows, w)
+        return total.reshape(len(zis), rows, w)
+
+    def owners(d):
+        if d == far:
+            return [lax.rem(z + far, nz)]
+        return [z] if d == 0 else [lax.rem(z + d, nz), lax.rem(z + nz - d, nz)]
+
+    def y_first(t, u):
+        return (t, u) in Y_FIRST
+
+    def yp_copy(k, d):
+        part = pl.ds(0, 1 if d in (0, far) else 2)
+        return rcopy(yps.at[k, d, part], ypr.at[k, d, part], yps_sem.at[k, d], ypr_sem.at[k, d], ypeer)
+
+    def zy_copy(direction, d, n):
+        to = (zright, zleft)[direction]
+        return rcopy(
+            zs.at[direction, d - 1, n, 0],
+            zr.at[direction, d - 1, n, 0],
+            zs_sem.at[direction, d - 1, n],
+            zr_sem.at[direction, d - 1, n],
+            to,
+        )
+
+    def column(t, u, who):
+        q = (half + t - 2 * half * t) * 2 + (core + who - 2 * core * who)
+        return pl.ds(pl.multiple_of((q * nu + u) * w, w), w)
+
+    def pre_step(t, u, who, d):
+        n, k = unit(t, u, who), Y_FIRST.index((t, u)) * 2 + who
+        p = product(n, owners(d), 1 - y).astype(jnp.bfloat16)
+        for j in range(p.shape[0]):
+            yps[k, d, j] = p[j]
+        yp_copy(k, d).start()
+
+    def step_y(t, u, who, d):
+        n, k = unit(t, u, who), Y_FIRST.index((t, u)) * 2 + who
+        p = product(n, owners(d), y)
+        yp_copy(k, d).wait_recv()
+        parts = [p[j] + ypr[k, d, j].astype(jnp.float32) for j in range(p.shape[0])]
+        if d == 0:
+            for direction in range(2):
+                zy_copy(direction, 1, n).wait_recv()
+                parts[0] = parts[0] + zr[direction, 0, n, 0].astype(jnp.float32)
+            out_ref[:, column(t, u, who)] = parts[0].astype(jnp.bfloat16)
+            return
+        for direction in (who,) if d == far else (0, 1):
+            part = parts[0 if d == far else direction]
+            if d + 1 < far or (d + 1 == far and direction == who):
+                zy_copy(direction, d + 1, n).wait_recv()
+                part = part + zr[direction, d, n, 0].astype(jnp.float32)
+            zs[direction, d - 1, n, 0] = part.astype(jnp.bfloat16)
+            zy_copy(direction, d, n).start()
 
     def step(n, d):
         if d == far:
@@ -260,35 +331,40 @@
             ys[n] = fin[n, 1 - y].astype(jnp.bfloat16)
             y_copy(n).start()
 
-    def phase(t, d):
-        def body(u, _):
-            step(unit(t, u, 0), d)
+    def arrived(t, u):
+        g_own(t, u, 2).wait_recv()
+        for i in range(4):
+            g_give(t, u, i).wait_recv()
+
+    def pre(t, u, d):
+        if y_first(t, u):
+            pre_step(t, u, 0, d)
             if d == far:
-                g_own(t, u, 2).wait_recv()
-                for i in range(4):
-                    g_give(t, u, i).wait_recv()
-            step(unit(t, u, 1), d)
-            return 0
-
-        lax.fori_loop(0, nu, body, 0)
+                arrived(t, u)
+            pre_step(t, u, 1, d)
+
+    def pair(t, u, d):
+        if y_first(t, u):
+            step_y(t, u, 0, d)
+            step_y(t, u, 1, d)
+            return
+        step(unit(t, u, 0), d)
+        if d == far:
+            arrived(t, u)
+        step(unit(t, u, 1), d)
 
     def finish(t):
-        def body(u, _):
+        for u in range(nu):
             for who in range(2):
-                n = unit(t, u, who)
-                y_copy(n).wait_recv()
-                q = (
-                    (half + t - 2 * half * t) * 2 + (core + who - 2 * core * who)
-                )
-                column = pl.multiple_of((q * nu + u) * w, w)
-                out_ref[:, pl.ds(column, w)] = (fin[n, y] + yr[n].astype(jnp.float32)).astype(jnp.bfloat16)
-            return 0
-
-        lax.fori_loop(0, nu, body, 0)
-
-    for c in og_copies:
+                if not y_first(t, u):
+                    n = unit(t, u, who)
+                    y_copy(n).wait_recv()
+                    out_ref[:, column(t, u, who)] = (fin[n, y] + yr[n].astype(jnp.float32)).astype(jnp.bfloat16)
+
+    og_copies[0].wait()
+    send_own(0, 0)
+    for c in og_copies[1:]:
         c.wait()
-    send_own(0)
 
     def cross_body(u, _):
         g_cross(u).start()
@@ -308,45 +384,114 @@
 
     lax.fori_loop(0, ncol, silu_body, 0)
 
-    h_send(0, 3)
-    relay(0)
-    h_relay(0, 3)
-    h_send(3, nz)
-    give_opp(0)
+    h_send(0, 1, (2, 3))
+    h_send(0, 1, (0, 1))
+    send_own(0, 1)
+    send_own(0, 2)
+    relay(0, 0)
+    h_relay(0, 1)
+    relay(0, 1)
+    send_own(1, 1)
+    h_send(1, 4, (2, 3))
+    relay(0, 2)
+    give_opp(0, 0)
+    h_send(4, 5, (2, 3))
+    h_send(1, 2, (0, 1))
     h_wait(0, 1)
-    phase(0, far)
+    pair(0, 0, 4)
+    h_send(2, 3, (0, 1))
+    give_opp(0, 1)
+    h_relay(1, 4)
+    pair(0, 1, 4)
+    h_send(3, 4, (0, 1))
+    give_opp(0, 2)
+    h_relay(4, 5)
+    relay(1, 1)
+    h_send(4, 5, (0, 1))
+    pair(0, 2, 4)
+    send_own(1, 2)
+    h_send(5, 7, (2, 3))
+    h_send(5, 6, (0, 1))
     h_wait(1, 3)
-    phase(0, far - 1)
-    h_relay(3, 5)
-    for d in range(far - 2, 0, -1):
-        o = 2 * (far - d) - 1
-        h_wait(o, o + 2)
-        phase(0, d)
-        if d == 2:
-            h_relay(5, nz)
-            send_own(1)
-    relay(1)
-    h_wait(nz - 1, nz)
-    phase(0, 0)
-    give_opp(1)
-    for d in range(far, -1, -1):
-        phase(1, d)
-        if d == far:
-            finish(0)
+    pair(0, 0, 3)
+    h_send(6, 7, (0, 1))
+    pair(0, 1, 3)
+    send_own(1, 0)
+    relay(1, 2)
+    pair(0, 2, 3)
+    h_relay(5, 7)
+    give_opp(1, 1)
+    h_send(7, 8, (2, 3))
+    h_wait(3, 5)
+    pair(0, 0, 2)
+    h_send(7, 8, (0, 1))
+    pre(1, 1, 4)
+    pre(1, 1, 3)
+    pre(1, 1, 2)
+    give_opp(1, 2)
+    pair(0, 1, 2)
+    relay(1, 0)
+    pair(1, 2, 4)
+    pair(0, 2, 2)
+    h_relay(7, 8)
+    h_wait(5, 7)
+    pre(1, 1, 1)
+    pair(1, 1, 4)
+    pair(0, 0, 1)
+    give_opp(1, 0)
+    pair(0, 1, 1)
+    h_wait(7, 8)
+    pre(1, 1, 0)
+    pre(1, 0, 4)
+    pre(1, 0, 3)
+    pre(1, 0, 2)
+    pair(1, 2, 3)
+    pre(1, 0, 1)
+    pair(1, 1, 3)
+    pair(0, 2, 1)
+    pre(1, 0, 0)
+    pair(0, 0, 0)
+    pair(1, 0, 4)
+    pair(0, 1, 0)
+    pair(1, 2, 2)
+    pair(1, 1, 2)
+    pair(0, 2, 0)
+    pair(1, 0, 3)
+    pair(1, 2, 1)
+    pair(1, 1, 1)
+    pair(1, 0, 2)
+    pair(1, 2, 0)
+    pair(1, 1, 0)
+    pair(1, 0, 1)
+    pair(1, 0, 0)
+    finish(0)
     finish(1)
 
-    def drain_g(u, _):
+    for u in range(nu):
         for t in range(2):
-            for i in range(3):
+            for i in (2,) if across(t, u) else (0, 1, 2):
                 g_own(t, u, i).wait_send()
-            for i in range(2):
+            for i in range(0 if across(t, u) else 2):
                 g_relay(t, u, i).wait_send()
             for i in range(4):
                 g_give(t, u, i).wait_send()
+            for i in range(4 if across(t, u) else 0):
+                g_across(u, i).wait_send()
+            for who in range(2):
+                n = unit(t, u, who)
+                if y_first(t, u):
+                    k = Y_FIRST.index((t, u)) * 2 + who
+                    for d in range(far + 1):
+                        yp_copy(k, d).wait_send()
+                    for d in range(1, far + 1):
+                        for direction in (who,) if d == far else (0, 1):
+                            zy_copy(direction, d, n).wait_send()
+                else:
+                    for d in range(1, far + 1):
+                        for direction in range(2):
+                            z_copy(direction, d, n).wait_send()
+                    y_copy(n).wait_send()
         g_cross(u).wait_send()
-        return 0
-
-    lax.fori_loop(0, nu, drain_g, 0)
 
     def drain_h(o, _):
         for i in range(6):
@@ -354,15 +499,6 @@
         return 0
 
     lax.fori_loop(0, nz, drain_h, 0)
-
-    def drain_z(n, _):
-        for d in range(1, far + 1):
-            for direction in range(2):
-                z_copy(direction, d, n).wait_send()
-        y_copy(n).wait_send()
-        return 0
-
-    lax.fori_loop(0, 4 * nu, drain_z, 0)
 
 
 def run(gate_pre, up_pre, out_grad, w=256, nz=NZ, interpret=False):
@@ -406,6 +542,12 @@
             dma((2, far, n)),
             dma((n,)),
             dma((n,)),
+            pltpu.VMEM((2 * len(Y_FIRST), far + 1, 2, rows, w), bf16),
+            pltpu.VMEM((2 * len(Y_FIRST), far + 1, 2, rows, w), bf16),
+            dma((2 * len(Y_FIRST), far + 1)),
+            dma((2 * len(Y_FIRST), far + 1)),
+            dma((4, nu)),
+            dma((4, nu)),
         ],
         compiler_params=pltpu.CompilerParams(
             collective_id=0, has_side_effects=True, vmem_limit_bytes=60 * 1024 * 1024

time: 90.8 us -> 75.8 us (0.83)
  Pallas kernels: 89 us -> 73.9 us
    pallas_call x1, Pallas kernels: 89 us -> 73.9 us  [run(): pl.pallas_call(functools.partial(kernel, (tb, rows, w, nu, nz)), out_shap...]
where the time goes in v2:
time: 75.8 us; the launch traced here: 75.6 us
  Pallas kernels  73.9 us (97%)
  local copies, waits for them, and re-layouts  1.69 us (2%)
    pallas_call x1, Pallas kernels, run(): pl.pallas_call(functools.partial(kernel, (tb, rows, w, nu, nz)), out_shap...  73.9 us
    unnamed x1, local copies, waits for them, and re-layouts  1.69 us

profile of v2, /device:TPU:8, one launch (start us, length us, event | category | flops | bytes accessed | tf_op | source)
XLA Modules:
  0.0 75.6 jit_solution(4466964375706529334)
XLA Ops:
  0.0 73.9 %shard_map.37 = bf16[48,3072]{1,0:T(8,128)(2,1)} custom-call(bf16[256,3072]{1,0:T(8,128)(2,1)} %gate_hbm.1, bf16[256,3072]{1,0:T(8,128)(2,1)} %up_hbm.1, bf16[256,768]{1,0:T(8,128)(2,1)} %og_hbm.1), custom_call_target="tpu_custom_call" | custom-call | tf_op jit(solution)/shard_map/pallas_call | solution.py:515
  73.9 1.7 %copy.5 = bf16[48,3072]{1,0:T(8,128)(2,1)} copy(bf16[48,3072]{1,0:T(8,128)(2,1)} %shard_map.37) | data formatting | bytes 589824

commit v3 on v2

--- a/solution.py
+++ b/solution.py
@@ -21,8 +21,7 @@
     up_hbm,
     og_hbm,
     out_ref,
-    gate,
-    up,
+    gu,
     ht,
     hbuf,
     hrel,
@@ -32,25 +31,22 @@
     fin,
     ys,
     yr,
+    yps,
+    ypr,
     loc_sem,
     og_sem,
-    gs_sem,
+    send_sem,
+    zsend_sem,
     gr_sem,
+    go_sem,
     gp_sem,
-    cs_sem,
     cr_sem,
-    hs_sem,
+    ca_sem,
+    hi_sem,
     hr_sem,
-    zs_sem,
     zr_sem,
-    ys_sem,
     yr_sem,
-    yps,
-    ypr,
-    yps_sem,
     ypr_sem,
-    cxs_sem,
-    cxr_sem,
 ):
     tb, rows, w, nu, nz = dims
     far = nz // 2
@@ -80,19 +76,17 @@
             src_ref=src, dst_ref=dst, send_sem=ssem, recv_sem=rsem, device_id=to, device_id_type=MESH
         )
 
-    ncol = gate.shape[0]
-    wide = gate.shape[2]
-    gate_copies = [
-        pltpu.make_async_copy(gate_hbm.at[:, pl.ds(i * wide, wide)], gate.at[i], loc_sem.at[0, i]) for i in range(ncol)
-    ]
-    up_copies = [
-        pltpu.make_async_copy(up_hbm.at[:, pl.ds(i * wide, wide)], up.at[i], loc_sem.at[1, i]) for i in range(ncol)
-    ]
+    ncol, _, _, wide = gu.shape
+    gu_copies = []
+    for i in range(ncol):
+        for j, source in enumerate((gate_hbm, up_hbm)):
+            part = source.at[:, pl.ds(i * wide, wide)]
+            gu_copies.append(pltpu.make_async_copy(part, gu.at[i, j], loc_sem.at[i]))
     og_copies = [
         pltpu.make_async_copy(og_hbm.at[:, pl.ds(u * w, w)], gbuf.at[unit(0, u, 0), OWN], og_sem.at[u])
         for u in range(nu)
     ]
-    for c in og_copies + gate_copies + up_copies:
+    for c in og_copies + gu_copies:
         c.start()
 
     barrier = pltpu.get_barrier_semaphore()
@@ -100,40 +94,48 @@
         pl.semaphore_signal(barrier, inc=1, device_id=peer, device_id_type=MESH)
     pl.semaphore_wait(barrier, len(peers))
 
+    def wait_in(ref, sem):
+        rcopy(ref, ref, sem, sem, partner).wait_recv()
+
+    def wait_out(ref, sem):
+        rcopy(ref, ref, sem, sem, partner).wait_send()
+
+    to_x, to_partner, to_cross, of_h, to_y, to_yp = (send_sem.at[i] for i in range(6))
+
     FIRST, LAST = pl.ds(0, half_t), pl.ds(half_t, half_t)
 
     def g_own(t, u, i):
         k = t * nu + u
         src = gbuf.at[unit(t, u, 0), OWN]
         if i == 0:
-            return rcopy(src, gbuf.at[unit(t, u, 0), LEFT], gs_sem.at[0, k], gr_sem.at[0, k], right)
+            return rcopy(src, gbuf.at[unit(t, u, 0), LEFT], to_x, gr_sem.at[k], right)
         if i == 1:
-            return rcopy(src, gbuf.at[unit(t, u, 0), RIGHT], gs_sem.at[1, k], gr_sem.at[1, k], left)
-        return rcopy(src, gbuf.at[unit(t, u, 1), OWN], gs_sem.at[2, k], gp_sem.at[0, k], partner)
+            return rcopy(src, gbuf.at[unit(t, u, 0), RIGHT], to_x, gr_sem.at[k], left)
+        return rcopy(src, gbuf.at[unit(t, u, 1), OWN], to_partner, gp_sem.at[k], partner)
 
     def g_relay(t, u, i):
         k = t * nu + u
         own = unit(t, u, 0)
         if i == 0:
             return rcopy(
-                gbuf.at[own, LEFT, FIRST], gbuf.at[own, OPP, FIRST], gs_sem.at[3, k], gr_sem.at[2, k], right
+                gbuf.at[own, LEFT, FIRST], gbuf.at[own, OPP, FIRST], to_x, go_sem.at[k], right
             )
-        return rcopy(gbuf.at[own, RIGHT, LAST], gbuf.at[own, OPP, LAST], gs_sem.at[4, k], gr_sem.at[3, k], left)
+        return rcopy(gbuf.at[own, RIGHT, LAST], gbuf.at[own, OPP, LAST], to_x, go_sem.at[k], left)
 
     def g_give(t, u, i):
         k = t * nu + u
         own, his = unit(t, u, 0), unit(t, u, 1)
         if i < 2:
             slot = (LEFT, RIGHT)[i]
-            return rcopy(gbuf.at[own, slot], gbuf.at[his, slot], gs_sem.at[5 + i, k], gp_sem.at[1 + i, k], partner)
+            return rcopy(gbuf.at[own, slot], gbuf.at[his, slot], to_partner, gp_sem.at[k], partner)
         part = (FIRST, LAST)[i - 2]
         return rcopy(
-            gbuf.at[own, OPP, part], gbuf.at[his, OPP, part], gs_sem.at[5 + i, k], gp_sem.at[1 + i, k], partner
+            gbuf.at[own, OPP, part], gbuf.at[his, OPP, part], to_partner, gp_sem.at[k], partner
         )
 
     def g_cross(u):
         return rcopy(
-            gbuf.at[unit(0, u, 0), OWN], gbuf.at[unit(1, u, 0), OWN], cs_sem.at[u], cr_sem.at[u], cross
+            gbuf.at[unit(0, u, 0), OWN], gbuf.at[unit(1, u, 0), OWN], to_cross, cr_sem.at[u], cross
         )
 
     def g_across(u, i):
@@ -144,7 +146,7 @@
         else:
             part = (FIRST, LAST)[i - 2]
             src, dst = gbuf.at[here, OPP, part], gbuf.at[there, OPP, part]
-        return rcopy(src, dst, cxs_sem.at[i, u], cxr_sem.at[i, u], cross)
+        return rcopy(src, dst, to_cross, ca_sem.at[i // 2, u], cross)
 
     def across(t, u):
         return t == 1 and u in ACROSS
@@ -156,22 +158,19 @@
             g_own(t, u, i).start()
 
     def relay(t, u):
+        own = gbuf.at[unit(t, u, 0)]
+        wait_in(own.at[pl.ds(LEFT, 2)], ca_sem.at[0, u] if across(t, u) else gr_sem.at[t * nu + u])
         for i in range(2):
-            if across(t, u):
-                g_across(u, i).wait_recv()
-            else:
-                g_own(t, u, i).wait_recv()
+            if not across(t, u):
                 g_relay(t, u, i).start()
             g_give(t, u, i).start()
             if across(1 - t, u):
                 g_across(u, i).start()
 
     def give_opp(t, u):
+        own = gbuf.at[unit(t, u, 0)]
+        wait_in(own.at[OPP], ca_sem.at[1, u] if across(t, u) else go_sem.at[t * nu + u])
         for i in range(2):
-            if across(t, u):
-                g_across(u, 2 + i).wait_recv()
-            else:
-                g_relay(t, u, i).wait_recv()
             g_give(t, u, 2 + i).start()
             if across(1 - t, u):
                 g_across(u, 2 + i).start()
@@ -197,7 +196,7 @@
             pair, to = (hrel.at[0, zi], hbuf.at[2, zi, 0]), right
         else:
             pair, to = (hrel.at[1, zi], hbuf.at[2, zi, 1]), left
-        return rcopy(pair[0], pair[1], hs_sem.at[i, o], hr_sem.at[i, o], to)
+        return rcopy(pair[0], pair[1], of_h, (hi_sem if i in (2, 3) else hr_sem).at[o], to)
 
     def h_send(lo, hi, kinds):
         def body(o, _):
@@ -209,8 +208,8 @@
 
     def h_relay(lo, hi):
         def body(o, _):
+            wait_in(hrel.at[:, z_of(o)], hi_sem.at[o])
             for i in range(2):
-                h_copy(o, 2 + i).wait_recv()
                 h_copy(o, 4 + i).start()
             return 0
 
@@ -218,8 +217,7 @@
 
     def h_wait(lo, hi):
         def body(o, _):
-            for i in (0, 1, 4, 5):
-                h_copy(o, i).wait_recv()
+            wait_in(hbuf.at[:, z_of(o)], hr_sem.at[o])
             return 0
 
         lax.fori_loop(lo, hi, body, 0)
@@ -230,10 +228,10 @@
             src, dst = zs.at[direction, d - 1, n, direction], zr.at[direction, d - 1, n, direction]
         else:
             src, dst = zs.at[direction, d - 1, n], zr.at[direction, d - 1, n]
-        return rcopy(src, dst, zs_sem.at[direction, d - 1, n], zr_sem.at[direction, d - 1, n], to)
+        return rcopy(src, dst, zsend_sem.at[0], zr_sem.at[d - 1, n // 2], to)
 
     def y_copy(n):
-        return rcopy(ys.at[n], yr.at[n], ys_sem.at[n], yr_sem.at[n], ypeer)
+        return rcopy(ys.at[n], yr.at[n], to_y, yr_sem.at[n // 2], ypeer)
 
     def lhs(slot, zi, yi):
         at_z = ht.at[x, zi] if slot == OWN else hbuf.at[slot - 1, zi]
@@ -260,15 +258,15 @@
 
     def yp_copy(k, d):
         part = pl.ds(0, 1 if d in (0, far) else 2)
-        return rcopy(yps.at[k, d, part], ypr.at[k, d, part], yps_sem.at[k, d], ypr_sem.at[k, d], ypeer)
+        return rcopy(yps.at[k, d, part], ypr.at[k, d, part], to_yp, ypr_sem.at[k // 2, d], ypeer)
 
     def zy_copy(direction, d, n):
         to = (zright, zleft)[direction]
         return rcopy(
             zs.at[direction, d - 1, n, 0],
             zr.at[direction, d - 1, n, 0],
-            zs_sem.at[direction, d - 1, n],
-            zr_sem.at[direction, d - 1, n],
+            zsend_sem.at[1],
+            zr_sem.at[d - 1, n // 2],
             to,
         )
 
@@ -286,18 +284,15 @@
     def step_y(t, u, who, d):
         n, k = unit(t, u, who), Y_FIRST.index((t, u)) * 2 + who
         p = product(n, owners(d), y)
-        yp_copy(k, d).wait_recv()
         parts = [p[j] + ypr[k, d, j].astype(jnp.float32) for j in range(p.shape[0])]
         if d == 0:
             for direction in range(2):
-                zy_copy(direction, 1, n).wait_recv()
                 parts[0] = parts[0] + zr[direction, 0, n, 0].astype(jnp.float32)
             out_ref[:, column(t, u, who)] = parts[0].astype(jnp.bfloat16)
             return
         for direction in (who,) if d == far else (0, 1):
             part = parts[0 if d == far else direction]
             if d + 1 < far or (d + 1 == far and direction == who):
-                zy_copy(direction, d + 1, n).wait_recv()
                 part = part + zr[direction, d, n, 0].astype(jnp.float32)
             zs[direction, d - 1, n, 0] = part.astype(jnp.bfloat16)
             zy_copy(direction, d, n).start()
@@ -311,7 +306,6 @@
         elif d > 0:
             p = product(n, [lax.rem(z + d, nz), lax.rem(z + nz - d, nz)])
             for direction in range(2):
-                z_copy(direction, d + 1, n).wait_recv()
                 if d + 1 == far:
                     zs[direction, d - 1, n, direction] = (
                         p[direction, direction] + zr[direction, d, n, direction].astype(jnp.float32)
@@ -325,16 +319,13 @@
         else:
             p = product(n, [z])[0]
             for direction in range(2):
-                z_copy(direction, 1, n).wait_recv()
                 p = p + zr[direction, 0, n].astype(jnp.float32)
             fin[n] = p
             ys[n] = fin[n, 1 - y].astype(jnp.bfloat16)
             y_copy(n).start()
 
     def arrived(t, u):
-        g_own(t, u, 2).wait_recv()
-        for i in range(4):
-            g_give(t, u, i).wait_recv()
+        wait_in(gbuf.at[unit(t, u, 1)], gp_sem.at[t * nu + u])
 
     def pre(t, u, d):
         if y_first(t, u):
@@ -343,8 +334,20 @@
                 arrived(t, u)
             pre_step(t, u, 1, d)
 
+    def z_in(t, u, d):
+        both = pl.ds(unit(t, u, 0), 2)
+        if y_first(t, u):
+            ref = zr.at[0, far - 1, both, 0] if d == far else zr.at[:, d - 1, both, 0]
+        else:
+            ref = zr.at[0, far - 1, both] if d == far else zr.at[:, d - 1, both]
+        wait_in(ref, zr_sem.at[d - 1, unit(t, u, 0) // 2])
+
     def pair(t, u, d):
+        if d < far:
+            z_in(t, u, d + 1)
         if y_first(t, u):
+            k = Y_FIRST.index((t, u))
+            wait_in(ypr.at[pl.ds(2 * k, 2), d, pl.ds(0, 1 if d in (0, far) else 2)], ypr_sem.at[k, d])
             step_y(t, u, 0, d)
             step_y(t, u, 1, d)
             return
@@ -355,11 +358,12 @@
 
     def finish(t):
         for u in range(nu):
+            if y_first(t, u):
+                continue
+            wait_in(yr.at[pl.ds(unit(t, u, 0), 2)], yr_sem.at[t * nu + u])
             for who in range(2):
-                if not y_first(t, u):
-                    n = unit(t, u, who)
-                    y_copy(n).wait_recv()
-                    out_ref[:, column(t, u, who)] = (fin[n, y] + yr[n].astype(jnp.float32)).astype(jnp.bfloat16)
+                n = unit(t, u, who)
+                out_ref[:, column(t, u, who)] = (fin[n, y] + yr[n].astype(jnp.float32)).astype(jnp.bfloat16)
 
     og_copies[0].wait()
     send_own(0, 0)
@@ -373,10 +377,9 @@
     lax.fori_loop(0, nu, cross_body, 0)
 
     def silu_body(i, _):
-        pltpu.make_async_copy(gate_hbm.at[:, pl.ds(pl.multiple_of(i * wide, 128), wide)], gate.at[i], loc_sem.at[0, i]).wait()
-        pltpu.make_async_copy(up_hbm.at[:, pl.ds(pl.multiple_of(i * wide, 128), wide)], up.at[i], loc_sem.at[1, i]).wait()
-        g = gate[i].astype(jnp.float32)
-        h = (g / (1.0 + jnp.exp(-g)) * up[i].astype(jnp.float32)).astype(jnp.bfloat16)
+        pltpu.make_async_copy(gu.at[i], gu.at[i], loc_sem.at[i]).wait()
+        g = gu[i, 0].astype(jnp.float32)
+        h = (g / (1.0 + jnp.exp(-g)) * gu[i, 1].astype(jnp.float32)).astype(jnp.bfloat16)
         ht[i // (nz * 2 * rows // wide), pl.ds(lax.rem(i, nz * 2 * rows // wide) * (wide // (2 * rows)), wide // (2 * rows))] = (
             h.T.reshape(wide // (2 * rows), 2, rows, tb)
         )
@@ -467,38 +470,15 @@
     finish(0)
     finish(1)
 
-    for u in range(nu):
-        for t in range(2):
-            for i in (2,) if across(t, u) else (0, 1, 2):
-                g_own(t, u, i).wait_send()
-            for i in range(0 if across(t, u) else 2):
-                g_relay(t, u, i).wait_send()
-            for i in range(4):
-                g_give(t, u, i).wait_send()
-            for i in range(4 if across(t, u) else 0):
-                g_across(u, i).wait_send()
-            for who in range(2):
-                n = unit(t, u, who)
-                if y_first(t, u):
-                    k = Y_FIRST.index((t, u)) * 2 + who
-                    for d in range(far + 1):
-                        yp_copy(k, d).wait_send()
-                    for d in range(1, far + 1):
-                        for direction in (who,) if d == far else (0, 1):
-                            zy_copy(direction, d, n).wait_send()
-                else:
-                    for d in range(1, far + 1):
-                        for direction in range(2):
-                            z_copy(direction, d, n).wait_send()
-                    y_copy(n).wait_send()
-        g_cross(u).wait_send()
-
-    def drain_h(o, _):
-        for i in range(6):
-            h_copy(o, i).wait_send()
-        return 0
-
-    lax.fori_loop(0, nz, drain_h, 0)
+    n_x, n_c, n_p = 2 * nu - len(ACROSS), 1 + len(ACROSS), len(Y_FIRST)
+    wait_out(gbuf.at[pl.ds(0, n_x), pl.ds(0, 3)], to_x)
+    wait_out(gbuf.at[pl.ds(0, 2 * nu)], to_partner)
+    wait_out(gbuf.at[pl.ds(0, n_c), pl.ds(0, 3)], to_cross)
+    wait_out(ht, of_h)
+    wait_out(zs.at[:, pl.ds(0, 2 * nu - n_p), pl.ds(0, 2 * far - 1)], zsend_sem.at[0])
+    wait_out(zs.at[0, pl.ds(0, n_p), pl.ds(0, 2 * far - 1)], zsend_sem.at[1])
+    wait_out(ys.at[pl.ds(0, 4 * nu - 2 * n_p)], to_y)
+    wait_out(yps.at[:, pl.ds(0, far)], to_yp)
 
 
 def run(gate_pre, up_pre, out_grad, w=256, nz=NZ, interpret=False):
@@ -518,8 +498,7 @@
         in_specs=[pl.BlockSpec(memory_space=pl.ANY)] * 3,
         out_specs=pl.BlockSpec(memory_space=pltpu.VMEM),
         scratch_shapes=[
-            pltpu.VMEM((ncol, tb, wide), bf16),
-            pltpu.VMEM((ncol, tb, wide), bf16),
+            pltpu.VMEM((ncol, 2, tb, wide), bf16),
             pltpu.VMEM((NX, nz, 2, rows, tb), bf16),
             pltpu.VMEM((3, nz, 2, rows, tb), bf16),
             pltpu.VMEM((2, nz, rows, tb), bf16),
@@ -529,25 +508,22 @@
             pltpu.VMEM((n, 2, rows, w), jnp.float32),
             pltpu.VMEM((n, rows, w), bf16),
             pltpu.VMEM((n, rows, w), bf16),
-            dma((2, ncol)),
-            dma((nu,)),
-            dma((9, 2 * nu)),
-            dma((4, 2 * nu)),
-            dma((5, 2 * nu)),
-            dma((nu,)),
-            dma((nu,)),
-            dma((6, nz)),
-            dma((6, nz)),
-            dma((2, far, n)),
-            dma((2, far, n)),
-            dma((n,)),
-            dma((n,)),
             pltpu.VMEM((2 * len(Y_FIRST), far + 1, 2, rows, w), bf16),
             pltpu.VMEM((2 * len(Y_FIRST), far + 1, 2, rows, w), bf16),
-            dma((2 * len(Y_FIRST), far + 1)),
-            dma((2 * len(Y_FIRST), far + 1)),
-            dma((4, nu)),
-            dma((4, nu)),
+            dma((ncol,)),
+            dma((nu,)),
+            dma((6,)),
+            dma((2,)),
+            dma((2 * nu,)),
+            dma((2 * nu,)),
+            dma((2 * nu,)),
+            dma((nu,)),
+            dma((2, nu)),
+            dma((nz,)),
+            dma((nz,)),
+            dma((far, 2 * nu)),
+            dma((2 * nu,)),
+            dma((len(Y_FIRST), far + 1)),
         ],
         compiler_params=pltpu.CompilerParams(
             collective_id=0, has_side_effects=True, vmem_limit_bytes=60 * 1024 * 1024

time: 75.8 us -> 73.8 us (0.974)
  Pallas kernels: 73.9 us -> 72 us
    pallas_call x1, Pallas kernels: 73.9 us -> 72 us  [run(): pl.pallas_call(functools.partial(kernel, (tb, rows, w, nu, nz)), out_shap...]
where the time goes in v3:
time: 73.8 us; the launch traced here: 73.7 us
  Pallas kernels  72 us (98%)
  local copies, waits for them, and re-layouts  1.69 us (2%)
    pallas_call x1, Pallas kernels, run(): pl.pallas_call(functools.partial(kernel, (tb, rows, w, nu, nz)), out_shap...  72 us
    unnamed x1, local copies, waits for them, and re-layouts  1.69 us

profile of v3, /device:TPU:8, one launch (start us, length us, event | category | flops | bytes accessed | tf_op | source)
XLA Modules:
  0.0 73.7 jit_solution(15354028702489777966)
XLA Ops:
  0.0 72.0 %shard_map.37 = bf16[48,3072]{1,0:T(8,128)(2,1)} custom-call(bf16[256,3072]{1,0:T(8,128)(2,1)} %gate_hbm.1, bf16[256,3072]{1,0:T(8,128)(2,1)} %up_hbm.1, bf16[256,768]{1,0:T(8,128)(2,1)} %og_hbm.1), custom_call_target="tpu_custom_call" | custom-call | tf_op jit(solution)/shard_map/pallas_call | solution.py:495
  72.0 1.7 %copy.5 = bf16[48,3072]{1,0:T(8,128)(2,1)} copy(bf16[48,3072]{1,0:T(8,128)(2,1)} %shard_map.37) | data formatting | bytes 589824

commit v4 on v3

--- a/solution.py
+++ b/solution.py
@@ -228,7 +228,7 @@
             src, dst = zs.at[direction, d - 1, n, direction], zr.at[direction, d - 1, n, direction]
         else:
             src, dst = zs.at[direction, d - 1, n], zr.at[direction, d - 1, n]
-        return rcopy(src, dst, zsend_sem.at[0], zr_sem.at[d - 1, n // 2], to)
+        return rcopy(src, dst, zsend_sem.at[0], zr_sem.at[d - 1, n], to)
 
     def y_copy(n):
         return rcopy(ys.at[n], yr.at[n], to_y, yr_sem.at[n // 2], ypeer)
@@ -258,7 +258,7 @@
 
     def yp_copy(k, d):
         part = pl.ds(0, 1 if d in (0, far) else 2)
-        return rcopy(yps.at[k, d, part], ypr.at[k, d, part], to_yp, ypr_sem.at[k // 2, d], ypeer)
+        return rcopy(yps.at[k, d, part], ypr.at[k, d, part], to_yp, ypr_sem.at[k, d], ypeer)
 
     def zy_copy(direction, d, n):
         to = (zright, zleft)[direction]
@@ -266,7 +266,7 @@
             zs.at[direction, d - 1, n, 0],
             zr.at[direction, d - 1, n, 0],
             zsend_sem.at[1],
-            zr_sem.at[d - 1, n // 2],
+            zr_sem.at[d - 1, n],
             to,
         )
 
@@ -274,16 +274,24 @@
         q = (half + t - 2 * half * t) * 2 + (core + who - 2 * core * who)
         return pl.ds(pl.multiple_of((q * nu + u) * w, w), w)
 
-    def pre_step(t, u, who, d):
+    def pre_step(t, u, who, ds):
         n, k = unit(t, u, who), Y_FIRST.index((t, u)) * 2 + who
-        p = product(n, owners(d), 1 - y).astype(jnp.bfloat16)
-        for j in range(p.shape[0]):
-            yps[k, d, j] = p[j]
-        yp_copy(k, d).start()
+        p = product(n, [zi for d in ds for zi in owners(d)], 1 - y).astype(jnp.bfloat16)
+        first = 0
+        for d in ds:
+            count = len(owners(d))
+            for j in range(count):
+                yps[k, d, j] = p[first + j]
+            yp_copy(k, d).start()
+            first += count
 
     def step_y(t, u, who, d):
         n, k = unit(t, u, who), Y_FIRST.index((t, u)) * 2 + who
         p = product(n, owners(d), y)
+        part = pl.ds(0, 1 if d in (0, far) else 2)
+        wait_in(ypr.at[k, d, part], ypr_sem.at[k, d])
+        if d < far:
+            wait_in(zr.at[who, d, n, 0] if d + 1 == far else zr.at[:, d, n, 0], zr_sem.at[d, n])
         parts = [p[j] + ypr[k, d, j].astype(jnp.float32) for j in range(p.shape[0])]
         if d == 0:
             for direction in range(2):
@@ -305,6 +313,7 @@
                 z_copy(direction, d, n).start()
         elif d > 0:
             p = product(n, [lax.rem(z + d, nz), lax.rem(z + nz - d, nz)])
+            wait_in(zr.at[0, d, n] if d + 1 == far else zr.at[:, d, n], zr_sem.at[d, n])
             for direction in range(2):
                 if d + 1 == far:
                     zs[direction, d - 1, n, direction] = (
@@ -318,6 +327,7 @@
                 z_copy(direction, d, n).start()
         else:
             p = product(n, [z])[0]
+            wait_in(zr.at[:, 0, n], zr_sem.at[0, n])
             for direction in range(2):
                 p = p + zr[direction, 0, n].astype(jnp.float32)
             fin[n] = p
@@ -327,27 +337,14 @@
     def arrived(t, u):
         wait_in(gbuf.at[unit(t, u, 1)], gp_sem.at[t * nu + u])
 
-    def pre(t, u, d):
+    def pre(t, u, *ds):
+        pre_step(t, u, 0, ds)
+        if far in ds:
+            arrived(t, u)
+        pre_step(t, u, 1, ds)
+
+    def pair(t, u, d):
         if y_first(t, u):
-            pre_step(t, u, 0, d)
-            if d == far:
-                arrived(t, u)
-            pre_step(t, u, 1, d)
-
-    def z_in(t, u, d):
-        both = pl.ds(unit(t, u, 0), 2)
-        if y_first(t, u):
-            ref = zr.at[0, far - 1, both, 0] if d == far else zr.at[:, d - 1, both, 0]
-        else:
-            ref = zr.at[0, far - 1, both] if d == far else zr.at[:, d - 1, both]
-        wait_in(ref, zr_sem.at[d - 1, unit(t, u, 0) // 2])
-
-    def pair(t, u, d):
-        if d < far:
-            z_in(t, u, d + 1)
-        if y_first(t, u):
-            k = Y_FIRST.index((t, u))
-            wait_in(ypr.at[pl.ds(2 * k, 2), d, pl.ds(0, 1 if d in (0, far) else 2)], ypr_sem.at[k, d])
             step_y(t, u, 0, d)
             step_y(t, u, 1, d)
             return
@@ -390,8 +387,8 @@
     h_send(0, 1, (2, 3))
     h_send(0, 1, (0, 1))
     send_own(0, 1)
+    relay(0, 0)
     send_own(0, 2)
-    relay(0, 0)
     h_relay(0, 1)
     relay(0, 1)
     send_own(1, 1)
@@ -428,9 +425,7 @@
     h_wait(3, 5)
     pair(0, 0, 2)
     h_send(7, 8, (0, 1))
-    pre(1, 1, 4)
-    pre(1, 1, 3)
-    pre(1, 1, 2)
+    pre(1, 1, 4, 3, 2)
     give_opp(1, 2)
     pair(0, 1, 2)
     relay(1, 0)
@@ -438,34 +433,30 @@
     pair(0, 2, 2)
     h_relay(7, 8)
     h_wait(5, 7)
+    pair(0, 0, 1)
     pre(1, 1, 1)
     pair(1, 1, 4)
-    pair(0, 0, 1)
     give_opp(1, 0)
     pair(0, 1, 1)
     h_wait(7, 8)
+    pre(1, 0, 4, 3, 2, 1, 0)
     pre(1, 1, 0)
-    pre(1, 0, 4)
-    pre(1, 0, 3)
-    pre(1, 0, 2)
     pair(1, 2, 3)
-    pre(1, 0, 1)
     pair(1, 1, 3)
     pair(0, 2, 1)
-    pre(1, 0, 0)
     pair(0, 0, 0)
     pair(1, 0, 4)
     pair(0, 1, 0)
     pair(1, 2, 2)
     pair(1, 1, 2)
+    pair(1, 0, 3)
     pair(0, 2, 0)
-    pair(1, 0, 3)
     pair(1, 2, 1)
+    pair(1, 0, 2)
     pair(1, 1, 1)
-    pair(1, 0, 2)
+    pair(1, 0, 1)
     pair(1, 2, 0)
     pair(1, 1, 0)
-    pair(1, 0, 1)
     pair(1, 0, 0)
     finish(0)
     finish(1)
@@ -521,9 +512,9 @@
             dma((2, nu)),
             dma((nz,)),
             dma((nz,)),
-            dma((far, 2 * nu)),
+            dma((far, n)),
             dma((2 * nu,)),
-            dma((len(Y_FIRST), far + 1)),
+            dma((2 * len(Y_FIRST), far + 1)),
         ],
         compiler_params=pltpu.CompilerParams(
             collective_id=0, has_side_effects=True, vmem_limit_bytes=60 * 1024 * 1024

time: 73.8 us -> 72.2 us (0.978)
  Pallas kernels: 72 us -> 70.4 us
    pallas_call x1, Pallas kernels: 72 us -> 70.4 us  [run(): pl.pallas_call(functools.partial(kernel, (tb, rows, w, nu, nz)), out_shap...]
where the time goes in v4:
time: 72.2 us; the launch traced here: 72.1 us
  Pallas kernels  70.4 us (98%)
  local copies, waits for them, and re-layouts  1.69 us (2%)
    pallas_call x1, Pallas kernels, run(): pl.pallas_call(functools.partial(kernel, (tb, rows, w, nu, nz)), out_shap...  70.4 us
    unnamed x1, local copies, waits for them, and re-layouts  1.69 us

profile of v4, /device:TPU:8, one launch (start us, length us, event | category | flops | bytes accessed | tf_op | source)
XLA Modules:
  0.0 72.1 jit_solution(17997289229106653634)
XLA Ops:
  0.0 70.4 %shard_map.37 = bf16[48,3072]{1,0:T(8,128)(2,1)} custom-call(bf16[256,3072]{1,0:T(8,128)(2,1)} %gate_hbm.1, bf16[256,3072]{1,0:T(8,128)(2,1)} %up_hbm.1, bf16[256,768]{1,0:T(8,128)(2,1)} %og_hbm.1), custom_call_target="tpu_custom_call" | custom-call | tf_op jit(solution)/shard_map/pallas_call | solution.py:486
  70.4 1.7 %copy.5 = bf16[48,3072]{1,0:T(8,128)(2,1)} copy(bf16[48,3072]{1,0:T(8,128)(2,1)} %shard_map.37) | data formatting | bytes 589824
